TPU v7x, 32 devices: a whole 2x2x4 slice. The times are simulated.
32 devices in a mesh: dp: 8 (over z, x), tensor: 4 (over y, core).
Axes of the slice: x: 2, y: 2, z: 4, core: 2. Of those that a mesh axis runs over, the one named last changes fastest.
Arguments:
- gradients: bfloat16 [8, 4096, 4096], P('dp', None, 'tensor'), may hold values from -300 to 300
- feedback: bfloat16 [8, 4096, 4096], P('dp', None, 'tensor'), may hold values from -12 to 12
- warm_start: float32 [4096, 64], P('tensor'), may hold values from -0.09375 to 0.09375
Outputs:
- projected: float32 [4096, 64], P('tensor')
- refreshed: float32 [4096, 64], P('tensor')
- decompressed: bfloat16 [4096, 4096], P(None, 'tensor')
All inputs are finite; a program needn't handle non-finite values.
Results may differ from a plain program's by a relative error of at most 0.001.
Values sent between devices are 32-bit elements; how exact they have to be, the bound alone decides.
A program may use at most 128 MiB of HBM per device.

v0:
```python
import jax
import jax.numpy as jnp
from jax import lax
from jax.sharding import PartitionSpec as P

HIGHEST = lax.Precision.HIGHEST


def on_device(gradients, feedback, warm_start):
    corrected = gradients[0].astype(jnp.float32) + feedback[0].astype(jnp.float32)
    members = lax.axis_size("dp")
    partial_value = lax.psum_scatter(
        jnp.dot(corrected, warm_start, precision=HIGHEST), "tensor", scatter_dimension=0, tiled=True
    )
    projected = lax.psum(partial_value, "dp") / members
    gram_matrix = lax.psum(jnp.dot(projected.T, projected, precision=HIGHEST), "tensor")
    factor = jnp.linalg.cholesky(gram_matrix)
    orth_shard = lax.linalg.triangular_solve(
        factor, projected, left_side=False, lower=True, transpose_a=True
    )
    basis = lax.all_gather(orth_shard, "tensor", axis=0, tiled=True)
    local_right = lax.dot_general(corrected, basis, (((0,), (0,)), ((), ())), precision=HIGHEST)
    refreshed = lax.psum(local_right, "dp") / members
    decompressed = jnp.dot(basis, refreshed.T, precision=HIGHEST).astype(jnp.bfloat16)
    return (projected, refreshed, decompressed)


def solution(mesh):
    return jax.shard_map(
        on_device,
        mesh=mesh,
        in_specs=(P("dp", None, "tensor"), P("dp", None, "tensor"), P("tensor", None)),
        out_specs=(P("tensor", None), P("tensor", None), P(None, "tensor")),
        check_vma=False,
    )
```

profile of v0, /device:TPU:0, one launch (start us, length us, event | category | flops | bytes accessed | tf_op | source)
XLA Modules:
  0.0 286.7 jit_solution(11949851245497997149)
XLA Ops:
  7.2 0.0 copy-start
  7.2 0.0 reduce-scatter.2.cloned.1.call-start
  7.2 0.9 copy-done
  8.1 22.3 %fusion.2 = f32[4096,64]{0,1:T(8,128)} fusion(f32[1024,64]{0,1:T(8,128)S(1)} %copy-done, bf16[1,4096,1024]{2,1,0:T(8,128)(2,1)} %param.4, bf16[1,4096,1024]{2,1,0:T(8,128)(2,1)} %param.3), kind=kOutput, calls=%fused_computation.2 | convolution fusion | flops 3233808384 | bytes 18087936 | tf_op jit(solution)/shard_map/dot_general | solution.py:13
  30.4 0.0 reduce-scatter.2.cloned.1.call-update
  30.5 0.0 all-reduce.3.cloned.1.call-start
  30.5 27.6 %reduce-scatter.2.cloned.1.call-done = f32[1024,64]{0,1:T(8,128)} async-done(((f32[4096,64]{0,1:T(8,128)}), f32[1024,64]{0,1:T(8,128)}) %reduce-scatter.2.cloned.1.call-update) | async-done | bytes 262160 | tf_op jit(solution)/shard_map/reduce_scatter | solution.py:12
  58.1 0.0 all-reduce.3.cloned.1.call-update
  58.1 0.0 all-gather.2.cloned.1.call-start
  58.2 74.3 %all-reduce.3.cloned.1.call-done = f32[1024,64]{0,1:T(8,128)} async-done(((f32[1024,64]{0,1:T(8,128)}), f32[1024,64]{0,1:T(8,128)}) %all-reduce.3.cloned.1.call-update) | async-done | bytes 262160 | tf_op jit(solution)/shard_map/psum | solution.py:15
  132.5 1.0 broadcast_multiply_fusion.1
  133.5 0.0 copy-start.2
  133.5 0.4 fusion.8
  133.9 10.3 %psum.22 = f32[64,64]{0,1:T(8,128)S(1)} all-reduce(f32[64,64]{0,1:T(8,128)S(1)} %fusion.8), channel_id=1, replica_groups=mesh['dp'=8,'tensor'=4] {'tensor'}, use_global_device_ids=true, to_apply=%region_2.0 | all-reduce | flops 4096 | bytes 32768 | tf_op jit(solution)/shard_map/psum | solution.py:16
  144.2 0.1 copy.7
  144.2 5.8 %cholesky.16 = f32[64,64]{1,0:T(8,128)S(1)} custom-call(f32[64,64]{1,0:T(8,128)S(1)} %fusion.7), custom_call_target="Cholesky" | custom-call | tf_op jit(solution)/shard_map/jit(cholesky)/cholesky | solution.py:17
  150.1 0.6 compare_reduce_fusion
  150.8 0.7 fusion.4
  151.4 4.9 %custom-call.6 = f32[1,64,64]{1,2,0:T(8,128)S(1)} custom-call(f32[1,64,64]{2,1,0:T(8,128)S(1)} %fusion.4), custom_call_target="InvertDiagBlocksLowerTriangular" | custom-call | tf_op jit(solution)/shard_map/triangular_solve | solution.py:18
  156.3 1.1 fusion.5
  157.5 0.0 all-gather.2.cloned.1.call-update
  157.5 0.2 all-reduce.5.cloned.1.call-start
  157.7 16.0 %all-gather.2.cloned.1.call-done = f32[4096,64]{0,1:T(8,128)} async-done(((f32[1024,64]{0,1:T(8,128)}), f32[4096,64]{0,1:T(8,128)}) %all-gather.2.cloned.1.call-update) | async-done | bytes 1048592 | tf_op jit(solution)/shard_map/all_gather | solution.py:21
  173.7 19.0 %fusion = f32[1024,64]{0,1:T(8,128)} fusion(f32[4096,64]{0,1:T(8,128)} %all-gather.2.cloned.1.call-done, bf16[1,4096,1024]{2,1,0:T(8,128)(2,1)} %param.4, bf16[1,4096,1024]{2,1,0:T(8,128)(2,1)} %param.3), kind=kOutput, calls=%fused_computation | convolution fusion | flops 3233808384 | bytes 18087936 | tf_op jit(solution)/shard_map/dot_general | solution.py:22
  192.7 0.0 copy-done.2
  192.7 0.0 all-reduce.5.cloned.1.call-update
  192.8 71.2 %all-reduce.5.cloned.1.call-done = f32[1024,64]{0,1:T(8,128)} async-done(((f32[1024,64]{0,1:T(8,128)}), f32[1024,64]{0,1:T(8,128)}) %all-reduce.5.cloned.1.call-update) | async-done | bytes 262160 | tf_op jit(solution)/shard_map/psum | solution.py:23
  263.9 1.0 broadcast_multiply_fusion
  264.9 0.0 copy-done.1
  264.9 0.0 copy-start.3
  264.9 15.3 %convolution_convert_fusion = bf16[4096,1024]{1,0:T(8,128)(2,1)} fusion(f32[4096,64]{0,1:T(8,128)S(1)} %copy-done.1, f32[1024,64]{0,1:T(8,128)S(1)} %broadcast_multiply_fusion), kind=kOutput, calls=%fused_computation.5 | convolution fusion | flops 3225419776 | bytes 9699328 | tf_op jit(solution)/shard_map/dot_general | solution.py:24
  280.2 0.0 copy-done.3
  (3 shorter events, 0.0 us)
Async XLA Ops:
  7.2 1.0 copy-start
  7.2 50.9 %reduce-scatter.2.cloned.1.call-start = ((), (), s32[]{:S(2)}) async-start(), calls=%async_computation.1 | async-start | bytes 1310720 | tf_op jit(solution)/shard_map/reduce_scatter | solution.py:12
  30.5 102.1 %all-reduce.3.cloned.1.call-start = ((), (), s32[]{:S(2)}) async-start(), calls=%async_computation.2 | async-start | bytes 524288 | tf_op jit(solution)/shard_map/psum | solution.py:15
  58.1 115.6 %all-gather.2.cloned.1.call-start = ((), (), s32[]{:S(2)}) async-start(), calls=%async_computation.3 | async-start | bytes 1310720 | tf_op jit(solution)/shard_map/all_gather | solution.py:21
  133.5 59.2 %copy-start.2 = (f32[1024,64]{0,1:T(8,128)}, f32[1024,64]{0,1:T(8,128)S(1)}, u32[]{:S(2)}) copy-start(f32[1024,64]{0,1:T(8,128)S(1)} %broadcast_multiply_fusion.1) | copy-start | bytes 786436
  157.5 106.4 %all-reduce.5.cloned.1.call-start = ((), (), s32[]{:S(2)}) async-start(), calls=%async_computation.4 | async-start | bytes 524288 | tf_op jit(solution)/shard_map/psum | solution.py:23
  173.7 91.2 %copy-start.1 = (f32[4096,64]{0,1:T(8,128)S(1)}, f32[4096,64]{0,1:T(8,128)}, u32[]{:S(2)}) copy-start(f32[4096,64]{0,1:T(8,128)} %all-gather.2.cloned.1.call-done) | copy-start | bytes 3145732
  264.9 15.3 %copy-start.3 = (f32[1024,64]{0,1:T(8,128)}, f32[1024,64]{0,1:T(8,128)S(1)}, u32[]{:S(2)}) copy-start(f32[1024,64]{0,1:T(8,128)S(1)} %broadcast_multiply_fusion) | copy-start | bytes 786436
Sparse Core Ops, SparseCore 0:
  30.6 27.4 reduce-scatter.1
  61.5 71.0 all-reduce.2
  157.6 16.0 all-gather.1
  192.9 71.0 all-reduce.4
where the time goes:
time: 287 us
  waiting for transfers between devices  189 us (66%)
  matrix products  58.1 us (20%)
  other arithmetic  14 us (5%)
  between operations  13.8 us (5%)
  blocking collectives  10.3 us (4%)
    psum x1, waiting for transfers between devices, on_device(): projected = lax.psum(partial_value, 'dp') / members  74.3 us
    psum x1, waiting for transfers between devices, on_device(): refreshed = lax.psum(local_right, 'dp') / members  71.2 us
    reduce_scatter x1, waiting for transfers between devices, on_device(): lax.psum_scatter(jnp.dot(corrected, warm_start, precision=HIGHEST), 'tens...  27.6 us
    dot_general x1, matrix products, on_device(): jnp.dot(corrected, warm_start, precision=HIGHEST)  22.3 us
    dot_general x1, matrix products, on_device(): lax.dot_general(corrected, basis, (((0,), (0,)), ((), ())), precision=HIG...  19 us
    all_gather x1, waiting for transfers between devices, on_device(): basis = lax.all_gather(orth_shard, 'tensor', axis=0, tiled=True)  16 us
    dot_general x1, matrix products, on_device(): jnp.dot(basis, refreshed.T, precision=HIGHEST).astype(jnp.bfloat16)  15.3 us
    psum x1, blocking collectives, on_device(): lax.psum(jnp.dot(projected.T, projected, precision=HIGHEST), 'tensor')  10.3 us
  transfers between devices with their start and end apart: 4, of which 4 were waited for; matrix products, arithmetic and copies ran while one was open for 0% of the time, Pallas kernels for 0%

commit v1 on v0

v1 whole, which is shorter than its diff:
```python
import functools

import jax
import jax.numpy as jnp
from jax import lax
from jax.experimental import pallas as pl
from jax.experimental.pallas import tpu as pltpu
from jax.sharding import PartitionSpec as P

MESH = pl.DeviceIdType.MESH
LANES = 128
SUBLANES = 8
MAX_CHUNKS = 4
BLOCK = 256


def pieces(x):
    high = x.astype(jnp.bfloat16)
    rest = x - high.astype(jnp.float32)
    middle = rest.astype(jnp.bfloat16)
    low = (rest - middle.astype(jnp.float32)).astype(jnp.bfloat16)
    return high, middle, low


def fold(x, rank):
    return x[:rank] + x[rank : 2 * rank] + x[2 * rank :]


def inverse_factor(gram, rank):
    row = lax.broadcasted_iota(jnp.int32, (rank, rank), 0)
    column = lax.broadcasted_iota(jnp.int32, (rank, rank), 1)
    both = jnp.concatenate([gram, jnp.where(row == column, 1.0, 0.0).astype(jnp.float32)], axis=1)
    below = lax.broadcasted_iota(jnp.int32, (rank, 1), 0)
    for k in range(rank - 1):
        pivot = both[k : k + 1, k : k + 1]
        scaled = both[k : k + 1, :] * (1.0 / pivot)
        both = both - jnp.where(below > k, both[:, k : k + 1], 0.0) * scaled
    diagonal = jnp.sum(jnp.where(row == column, both[:, :rank], 0.0), axis=1, keepdims=True)
    return both[:, rank:] * (1.0 / jnp.sqrt(diagonal))


def sum_kernel(
    members, tensors, chunks,
    g_hbm, f_hbm, w_ref, own_ref, basis_ref, right_ref,
    g_ref, f_ref, w3_ref, p3_ref, part, acc_core, acc_y, full, recv_core, recv_y, recv_dp,
    right_part, right_full, recv_right, macc, gram_ref,
    load_sem, core_s, core_r, y_s, y_r, dp_s, dp_r, gd_s, gd_r, gy_s, gy_r, gc_s, gc_r,
    ms_s, ms_r, mg_s, mg_r,
):
    depth, width = g_hbm.shape
    rank = w_ref.shape[1]
    ys = tensors // 2
    columns = depth // chunks
    rows = part.shape[0] // chunks
    half, quarter = rows // 2, rows // 2 // ys
    piece = quarter // members
    me = lax.axis_index("dp")
    mine = lax.axis_index("tensor")
    y, core = lax.div(mine, 2), lax.rem(mine, 2)
    partner = y * 2 + (1 - core)

    def member(k):
        return lax.rem(me + k, members)

    def along(k):
        return lax.rem(y + k, ys)

    def dp_device(k):
        return {"dp": member(k), "tensor": mine}

    def y_device(k):
        return {"dp": me, "tensor": along(k) * 2 + core}

    core_device = {"dp": me, "tensor": partner}

    def at(start, size):
        return pl.ds(pl.multiple_of(start, SUBLANES), size)

    def remote(source, target, send, receive, device):
        copy = pltpu.make_async_remote_copy(
            src_ref=source, dst_ref=target, send_sem=send, recv_sem=receive,
            device_id=device, device_id_type=MESH,
        )
        copy.start()
        return copy

    loads = []
    for j in range(chunks):
        here = pl.ds(j * columns, columns)
        pair = [
            pltpu.make_async_copy(g_hbm.at[here], g_ref.at[here], load_sem.at[j, 0]),
            pltpu.make_async_copy(f_hbm.at[here], f_ref.at[here], load_sem.at[j, 1]),
        ]
        for copy in pair:
            copy.start()
        loads.append(pair)

    barrier = pltpu.get_barrier_semaphore()
    partners = [core_device] + [y_device(k) for k in range(1, ys)] + [dp_device(k) for k in range(1, members)]
    for device in partners:
        pl.semaphore_signal(barrier, inc=1, device_id=device, device_id_type=MESH)

    for i, w in enumerate(pieces(w_ref[...].T)):
        w3_ref[i * rank : (i + 1) * rank, :] = w
    pl.semaphore_wait(barrier, len(partners))

    sends = []
    state = [dict() for _ in range(chunks)]

    def project(j):
        for copy in loads[j]:
            copy.wait()
        for b in range(columns // BLOCK):
            here = pl.ds(j * columns + b * BLOCK, BLOCK)
            dims = (((1,), (1,)), ((), ()))
            value = lax.dot_general(w3_ref[...], g_ref[here, :], dims, preferred_element_type=jnp.float32)
            value += lax.dot_general(w3_ref[...], f_ref[here, :], dims, preferred_element_type=jnp.float32)
            value = fold(value, rank)
            for i in range(BLOCK // LANES):
                first = j * rows + (b * (BLOCK // LANES) + i) * rank
                part[first : first + rank, :] = value[:, i * LANES : (i + 1) * LANES]
        state[j]["core"] = remote(
            part.at[at(j * rows + (1 - core) * half, half)], recv_core.at[pl.ds(j * half, half)],
            core_s.at[j], core_r.at[j], core_device,
        )

    def add_core(j):
        copy = state[j]["core"]
        copy.wait_recv()
        sends.append(copy)
        acc_core[j * half : (j + 1) * half, :] = (
            part[at(j * rows + core * half, half), :] + recv_core[j * half : (j + 1) * half, :]
        )
        state[j]["y"] = [
            remote(
                acc_core.at[at(j * half + along(k) * quarter, quarter)], recv_y.at[j, k],
                y_s.at[j, k], y_r.at[j, k], y_device(k),
            )
            for k in range(1, ys)
        ]

    def add_y(j):
        total = acc_core[at(j * half + y * quarter, quarter), :]
        for k, copy in enumerate(state[j]["y"], 1):
            copy.wait_recv()
            sends.append(copy)
            total += recv_y[j, k]
        acc_y[j * quarter : (j + 1) * quarter, :] = total
        state[j]["dp"] = [
            remote(
                acc_y.at[at(j * quarter + member(k) * piece, piece)], recv_dp.at[j, k],
                dp_s.at[j, k], dp_r.at[j, k], dp_device(k),
            )
            for k in range(1, members)
        ]

    def add_dp(j):
        total = acc_y[at(j * quarter + me * piece, piece), :]
        for k, copy in enumerate(state[j]["dp"], 1):
            copy.wait_recv()
            sends.append(copy)
            total += recv_dp[j, k]
        here = at(j * rows + core * half + y * quarter + me * piece, piece)
        full[here, :] = total * (1.0 / members)
        state[j]["gd"] = [
            remote(full.at[here], full.at[here], gd_s.at[j, k], gd_r.at[j, k], dp_device(k))
            for k in range(1, members)
        ]

    def gather_y(j):
        for copy in state[j]["gd"]:
            copy.wait_recv()
            sends.append(copy)
        here = at(j * rows + core * half + y * quarter, quarter)
        state[j]["gy"] = [
            remote(full.at[here], full.at[here], gy_s.at[j, k], gy_r.at[j, k], y_device(k))
            for k in range(1, ys)
        ]

    def gather_core(j):
        for copy in state[j]["gy"]:
            copy.wait_recv()
            sends.append(copy)
        here = at(j * rows + core * half, half)
        state[j]["gc"] = remote(full.at[here], full.at[here], gc_s.at[j], gc_r.at[j], core_device)

    def multiply(j):
        copy = state[j]["gc"]
        copy.wait_recv()
        sends.append(copy)
        for i in range(columns // LANES):
            first = j * rows + i * rank
            for q, p in enumerate(pieces(full[first : first + rank, :])):
                p3_ref[q * rank : (q + 1) * rank, i * LANES : (i + 1) * LANES] = p
        p3 = p3_ref[...]
        square = lax.dot_general(p3, p3, (((1,), (1,)), ((), ())), preferred_element_type=jnp.float32)
        square = fold(square, rank)
        square = square[:, :rank] + square[:, rank : 2 * rank] + square[:, 2 * rank :]
        gram_ref[...] = square if j == 0 else gram_ref[...] + square
        here = pl.ds(j * columns, columns)
        for b in range(width // BLOCK):
            cols = slice(b * BLOCK, (b + 1) * BLOCK)
            value = jnp.dot(p3_ref[...], g_ref[here, cols], preferred_element_type=jnp.float32)
            value += jnp.dot(p3_ref[...], f_ref[here, cols], preferred_element_type=jnp.float32)
            value = fold(value, rank)
            macc[:, cols] = value if j == 0 else macc[:, cols] + value

    stages = [project, add_core, add_y, add_dp, gather_y, gather_core, multiply]
    for step in range(chunks + len(stages) - 1):
        for s in reversed(range(len(stages))):
            if 0 <= step - s < chunks:
                stages[s](step - s)

    groups = width // LANES
    for i in range(groups):
        right_part[i * rank : (i + 1) * rank, :] = macc[:, i * LANES : (i + 1) * LANES]
    share = groups * rank // members
    copies = [
        remote(
            right_part.at[at(member(k) * share, share)], recv_right.at[k],
            ms_s.at[k], ms_r.at[k], dp_device(k),
        )
        for k in range(1, members)
    ]
    inverse = inverse_factor(gram_ref[...], rank)
    total = right_part[at(me * share, share), :]
    for k, copy in enumerate(copies, 1):
        copy.wait_recv()
        sends.append(copy)
        total += recv_right[k]
    here = at(me * share, share)
    right_full[here, :] = total * (1.0 / members)
    copies = [
        remote(right_full.at[here], right_full.at[here], mg_s.at[k], mg_r.at[k], dp_device(k))
        for k in range(1, members)
    ]

    for i in range(depth // LANES):
        value = jnp.dot(
            inverse, full[i * rank : (i + 1) * rank, :],
            precision=lax.Precision.HIGHEST, preferred_element_type=jnp.float32,
        )
        high, middle, _ = pieces(value)
        cols = slice(i * LANES, (i + 1) * LANES)
        basis_ref[:rank, cols] = high
        basis_ref[rank : 2 * rank, cols] = middle
        basis_ref[2 * rank :, cols] = high
    own_ref[...] = full[at(mine * (groups * rank), groups * rank), :]

    for copy in copies:
        copy.wait_recv()
        sends.append(copy)
    for i in range(groups):
        right_ref[:, i * LANES : (i + 1) * LANES] = jnp.dot(
            inverse, right_full[i * rank : (i + 1) * rank, :],
            precision=lax.Precision.HIGHEST, preferred_element_type=jnp.float32,
        )
    for copy in sends:
        copy.wait_send()


def expand_kernel(own_ref, basis_ref, right_ref, projected_ref, refreshed_ref, out_ref, r3_ref):
    rank, width = right_ref.shape

    @pl.when(pl.program_id(0) == 0)
    def _():
        high, middle, _ = pieces(right_ref[...])
        r3_ref[:rank] = high
        r3_ref[rank : 2 * rank] = high
        r3_ref[2 * rank :] = middle
        refreshed_ref[...] = right_ref[...].T
        for i in range(width // LANES):
            projected_ref[i * LANES : (i + 1) * LANES, :] = own_ref[i * rank : (i + 1) * rank, :].T

    out_ref[...] = lax.dot_general(
        basis_ref[...], r3_ref[...], (((0,), (0,)), ((), ())), preferred_element_type=jnp.float32
    ).astype(out_ref.dtype)


def on_device(members, tensors, gradients, feedback, warm_start):
    _, depth, width = gradients.shape
    rank = warm_start.shape[1]
    total_rows = depth * rank // LANES
    chunks = max(1, min(MAX_CHUNKS, total_rows // (SUBLANES * members * tensors)))
    columns = depth // chunks
    rows = total_rows // chunks
    half = rows // 2
    ys = tensors // 2
    quarter = half // ys
    piece = quarter // members
    groups = width // LANES
    share = groups * rank // members
    f32, bf16 = jnp.float32, jnp.bfloat16
    dma = pltpu.SemaphoreType.DMA
    vmem = pl.BlockSpec(memory_space=pltpu.VMEM)
    own, basis, right = pl.pallas_call(
        functools.partial(sum_kernel, members, tensors, chunks),
        out_shape=(
            jax.ShapeDtypeStruct((groups * rank, LANES), f32),
            jax.ShapeDtypeStruct((3 * rank, depth), bf16),
            jax.ShapeDtypeStruct((rank, width), f32),
        ),
        in_specs=[pl.BlockSpec(memory_space=pl.ANY)] * 2 + [vmem],
        out_specs=(vmem, vmem, vmem),
        scratch_shapes=[
            pltpu.VMEM((depth, width), bf16),
            pltpu.VMEM((depth, width), bf16),
            pltpu.VMEM((3 * rank, width), bf16),
            pltpu.VMEM((3 * rank, columns), bf16),
            pltpu.VMEM((total_rows, LANES), f32),
            pltpu.VMEM((total_rows // 2, LANES), f32),
            pltpu.VMEM((total_rows // 2 // ys, LANES), f32),
            pltpu.VMEM((total_rows, LANES), f32),
            pltpu.VMEM((total_rows // 2, LANES), f32),
            pltpu.VMEM((chunks, ys, quarter, LANES), f32),
            pltpu.VMEM((chunks, members, piece, LANES), f32),
            pltpu.VMEM((groups * rank, LANES), f32),
            pltpu.VMEM((groups * rank, LANES), f32),
            pltpu.VMEM((members, share, LANES), f32),
            pltpu.VMEM((rank, width), f32),
            pltpu.VMEM((rank, rank), f32),
            dma((chunks, 2)),
            dma((chunks,)), dma((chunks,)),
            dma((chunks, ys)), dma((chunks, ys)),
            dma((chunks, members)), dma((chunks, members)),
            dma((chunks, members)), dma((chunks, members)),
            dma((chunks, ys)), dma((chunks, ys)),
            dma((chunks,)), dma((chunks,)),
            dma((members,)), dma((members,)),
            dma((members,)), dma((members,)),
        ],
        compiler_params=pltpu.CompilerParams(
            collective_id=0, has_side_effects=True, vmem_limit_bytes=48 * 2**20
        ),
    )(gradients[0], feedback[0], warm_start)

    block = min(512, depth)
    return pl.pallas_call(
        expand_kernel,
        grid=(depth // block,),
        out_shape=(
            jax.ShapeDtypeStruct((width, rank), f32),
            jax.ShapeDtypeStruct((width, rank), f32),
            jax.ShapeDtypeStruct((depth, width), bf16),
        ),
        in_specs=[
            pl.BlockSpec((groups * rank, LANES), lambda i: (0, 0)),
            pl.BlockSpec((3 * rank, block), lambda i: (0, i)),
            pl.BlockSpec((rank, width), lambda i: (0, 0)),
        ],
        out_specs=(
            pl.BlockSpec((width, rank), lambda i: (0, 0)),
            pl.BlockSpec((width, rank), lambda i: (0, 0)),
            pl.BlockSpec((block, width), lambda i: (i, 0)),
        ),
        scratch_shapes=[pltpu.VMEM((3 * rank, width), bf16)],
        compiler_params=pltpu.CompilerParams(dimension_semantics=("arbitrary",)),
    )(own, basis, right)


def solution(mesh):
    return jax.shard_map(
        functools.partial(on_device, mesh.shape["dp"], mesh.shape["tensor"]),
        mesh=mesh,
        in_specs=(P("dp", None, "tensor"), P("dp", None, "tensor"), P("tensor", None)),
        out_specs=(P("tensor", None), P("tensor", None), P(None, "tensor")),
        check_vma=False,
    )
```

time: 287 us -> 72.4 us (0.25)
  waiting for transfers between devices: 189 us -> 0 us
  Pallas kernels: 0 us -> 63.8 us
  matrix products: 58.1 us -> 0 us
  other arithmetic: 14 us -> 0 us
  between operations: 13.8 us -> 0.66 us
  blocking collectives: 10.3 us -> 0 us
  local copies, waits for them, and re-layouts: 0.99 us -> 7.56 us
    psum x2 -> x0, waiting for transfers between devices: 146 us -> none  [the longest x1 74.3 us: on_device(): projected = lax.psum(partial_value, 'dp') / members]
    pallas_call x0 -> x2, Pallas kernels: none -> 63.8 us  [the longest x1 54.9 us: on_device(): pl.pallas_call(functools.partial(sum_kernel, members, tensors, chunks), o...]
    dot_general x4 -> x0, matrix products: 57 us -> none  [the longest x1 22.3 us: on_device(): jnp.dot(corrected, warm_start, precision=HIGHEST)]
    reduce_scatter x1 -> x0, waiting for transfers between devices: 27.6 us -> none  [on_device(): lax.psum_scatter(jnp.dot(corrected, warm_start, precision=HIGHEST), 'tens...]
    all_gather x1 -> x0, waiting for transfers between devices: 16 us -> none  [on_device(): basis = lax.all_gather(orth_shard, 'tensor', axis=0, tiled=True)]
    another operation x5 -> x0, other arithmetic: 12.1 us -> none  [the longest x3 6.52 us: on_device(): factor = jnp.linalg.cholesky(gram_matrix)]
    psum x1 -> x0, blocking collectives: 10.3 us -> none  [on_device(): lax.psum(jnp.dot(projected.T, projected, precision=HIGHEST), 'tensor')]
    pallas_call x0 -> x2, local copies, waits for them, and re-layouts: none -> 3.85 us  [on_device(): pl.pallas_call(expand_kernel, grid=(depth // block,), out_shape=(jax.Shap...]
  transfers between devices with their start and end apart: 4 -> 0, of which waited for: 4 -> 0; matrix products, arithmetic and copies ran while one was open for 0% -> 0% of each run, Pallas kernels for 0% -> 0%
where the time goes in v1:
time: 72.4 us; the launch traced here: 72 us
  Pallas kernels  63.8 us (88%)
  local copies, waits for them, and re-layouts  7.56 us (10%)
    pallas_call x1, Pallas kernels, on_device(): pl.pallas_call(functools.partial(sum_kernel, members, tensors, chunks), o...  54.9 us
    pallas_call x1, Pallas kernels, on_device(): pl.pallas_call(expand_kernel, grid=(depth // block,), out_shape=(jax.Shap...  8.92 us
    pallas_call x2, local copies, waits for them, and re-layouts, on_device(): pl.pallas_call(expand_kernel, grid=(depth // block,), out_shape=(jax.Shap...  3.85 us
    unnamed x7, local copies, waits for them, and re-layouts  3.7 us

profile of v1, /device:TPU:0, one launch (start us, length us, event | category | flops | bytes accessed | tf_op | source)
XLA Modules:
  0.0 72.0 jit_solution(12670396133017609005)
XLA Ops:
  0.6 1.1 %copy.6.w_ref = f32[1024,64]{1,0:T(8,128)S(1)} copy(f32[1024,64]{0,1:T(8,128)} %param.5) | data formatting | bytes 524288 | tf_op args[2]
  1.8 54.9 %shard_map.58 = (f32[512,128]{1,0:T(8,128)S(1)}, bf16[192,4096]{1,0:T(8,128)(2,1)S(1)}, f32[64,1024]{1,0:T(8,128)S(1)}) custom-call(bf16[4096,1024]{1,0:T(8,128)(2,1)} %bitcast.2, bf16[4096,1024]{1,0:T(8,128)(2,1)} %bitcast.3, f32[1024,64]{1,0:T(8,128)S(1)} %copy.6.w_ref), custom_call_target="tpu_custom_call" | custom-call | tf_op jit(solution)/shard_map/pallas_call | solution.py:296
  56.7 0.0 copy-start
  56.7 1.2 %copy-done = bf16[192,4096]{1,0:T(8,128)(2,1)} copy-done((bf16[192,4096]{1,0:T(8,128)(2,1)}, bf16[192,4096]{1,0:T(8,128)(2,1)S(1)}, u32[]{:S(2)}) %copy-start) | copy-done | bytes 1572888
  57.9 0.0 copy-start.1
  57.9 0.7 copy-done.1
  58.6 0.0 copy-start.2
  58.6 0.7 copy-done.2
  59.3 8.9 %shard_map.59 = (f32[1024,64]{1,0:T(8,128)}, f32[1024,64]{1,0:T(8,128)}, bf16[4096,1024]{1,0:T(8,128)(2,1)}) custom-call(f32[512,128]{1,0:T(8,128)} %copy-done.1, bf16[192,4096]{1,0:T(8,128)(2,1)} %copy-done, f32[64,1024]{1,0:T(8,128)} %copy-done.2), custom_call_target="tpu_custom_call" | custom-call | tf_op jit(solution)/shard_map/pallas_call | solution.py:338
  68.2 1.9 %copy.7 = f32[1024,64]{0,1:T(8,128)} copy(f32[1024,64]{1,0:T(8,128)} %get-tuple-element.9) | data formatting | bytes 524288 | tf_op jit(solution)/shard_map/pallas_call | solution.py:338
  70.1 1.9 %copy.8 = f32[1024,64]{0,1:T(8,128)} copy(f32[1024,64]{1,0:T(8,128)} %get-tuple-element.10) | data formatting | bytes 524288 | tf_op jit(solution)/shard_map/pallas_call | solution.py:338
Async XLA Ops:
  56.7 1.2 %copy-start = (bf16[192,4096]{1,0:T(8,128)(2,1)}, bf16[192,4096]{1,0:T(8,128)(2,1)S(1)}, u32[]{:S(2)}) copy-start(bf16[192,4096]{1,0:T(8,128)(2,1)S(1)} %get-tuple-element.7.basis_ref) | copy-start | bytes 4718596
  57.9 0.7 copy-start.1
  58.6 0.7 copy-start.2
